TPU v7x, 512 devices: a whole 4x8x8 slice. The times are simulated.
512 devices in a mesh: wide: 64 (over y_hi, z, x), narrow: 8 (over y_lo, core).
Axes of the slice: x: 4, y: 8 (y_hi: 2, y_lo: 4; y = y_hi * 4 + y_lo), z: 8, core: 2. Of those that a mesh axis runs over, the one named last changes fastest.
Arguments:
- hidden_in: bfloat16 [16384, 2048], P('wide', 'narrow'), may hold values from -32 to 32
- attn_gain: bfloat16 [2048], P('narrow'), may hold values from 0.099609375 to 1.8984375
- qkv_weight: bfloat16 [2048, 1920], P('narrow', 'wide'), may hold values from -0.125 to 0.125
- q_gain: bfloat16 [64], replicated, may hold values from 1 to 2
- k_gain: bfloat16 [64], replicated, may hold values from 1 to 2
- out_weight: bfloat16 [1280, 2048], P('wide', 'narrow'), may hold values from -0.3125 to 0.3125
- lengths: int32 [4], replicated, may hold values from 1 to 8192, 16384 in all
- page_table: int32 [256], P('wide'), may hold values from 0 to 3, as said below
Outputs:
- hidden_out: bfloat16 [16384, 2048], P('wide', 'narrow')
- kv_cache: bfloat16 [256, 64, 640], P('wide', 'narrow')
Inputs may be any that keep to these rules, and one draw needn't show every extreme that they name: `lengths`: the 4 prompts sum to 16384 tokens and the longest has exactly 8192. `page_table`: each aligned block of 4 entries holds each slot once.
All inputs are finite; a program needn't handle non-finite values.
Results may differ from a plain program's by a relative error of at most 0.0033.
The roundings to bfloat16 on the way count: a program that leaves them out, or rounds other values in their place, can miss the bound.
Values may be sent and summed in bfloat16 or wider, within the bound.
No kernel may reach another device: no remote copies, remote signals or barrier semaphores. Data moves between devices by JAX's collectives and lax.ppermute only.
A program may use at most 128 MiB of HBM per device.

v0:
```python
import math
import jax
import jax.numpy as jnp
from jax import lax
from jax.sharding import PartitionSpec as P

D = 2048
HEADS = 20
KV_HEADS = 5
HEAD = 64
PAGE = 64
GROUP = 4
Q_DIM = 1280
KV_DIM = 640
rope_base = 10000.0


def token_place(token_ids, lengths):
    prompt_ends = jnp.cumsum(lengths)
    prompt_starts = prompt_ends - lengths
    segment = jnp.sum((token_ids[:, None] >= prompt_ends[None, :]).astype(jnp.int32), axis=1)
    matches = segment[:, None] == jnp.arange(lengths.shape[0], dtype=jnp.int32)[None, :]
    position = token_ids - jnp.sum(jnp.where(matches, prompt_starts[None, :], 0), axis=1)
    return (segment, position)


def rotate(projected_part, head_count, head_gain, position):
    row_count = projected_part.shape[0]
    per_head = projected_part.reshape(row_count, head_count, HEAD)
    per_head = per_head * lax.rsqrt(jnp.mean(per_head * per_head, axis=-1, keepdims=True) + 1e-06)
    per_head = per_head * head_gain.astype(jnp.float32)
    halfway = HEAD // 2
    frequency = jnp.exp(
        jnp.arange(halfway, dtype=jnp.float32) * (-2.0 * math.log(rope_base) / HEAD)
    )
    angles = position.astype(jnp.float32)[:, None] * frequency[None, :]
    cosine_table = jnp.cos(angles)[:, None, :]
    sine_table = jnp.sin(angles)[:, None, :]
    lower_half = per_head[..., :halfway]
    upper_half = per_head[..., halfway:]
    rotated = jnp.concatenate(
        [
            lower_half * cosine_table - upper_half * sine_table,
            upper_half * cosine_table + lower_half * sine_table,
        ],
        axis=-1,
    )
    return rotated.reshape(row_count, head_count * HEAD)


def on_device(hidden_in, attn_gain, qkv_weight, q_gain, k_gain, out_weight, lengths, page_table):
    tokens_dev = hidden_in.shape[0]
    narrow_count = lax.axis_size("narrow")
    narrow_index = lax.axis_index("narrow")
    wide_index = lax.axis_index("wide")
    rows_page = PAGE // narrow_count
    pages_dev = tokens_dev // PAGE
    slice_rows = pages_dev * rows_page
    key_width = KV_DIM // 2
    scale = HEAD ** (-0.5)
    input_values = hidden_in.astype(jnp.float32)
    scaled = (input_values * attn_gain.astype(jnp.float32)[None, :]).astype(jnp.bfloat16)
    square_part = jnp.sum(input_values * input_values, axis=1)
    partial_sums = jnp.dot(
        scaled,
        lax.all_gather(qkv_weight, "wide", axis=1, tiled=True),
        preferred_element_type=jnp.float32,
    )
    first_token = wide_index * tokens_dev
    all_tokens = first_token + jnp.arange(tokens_dev, dtype=jnp.int32)
    own_tokens = (
        first_token
        + jnp.arange(pages_dev, dtype=jnp.int32)[:, None] * PAGE
        + narrow_index * rows_page
        + jnp.arange(rows_page, dtype=jnp.int32)[None, :]
    ).reshape(-1)
    segment_all, position_all = token_place(all_tokens, lengths)
    segment_own, position_own = token_place(own_tokens, lengths)
    summed, squares = lax.psum((partial_sums, square_part), "narrow")
    inverse_norm = lax.rsqrt(squares / D + 1e-06)
    projected = summed * inverse_norm[:, None]
    queries = rotate(projected[:, :Q_DIM], HEADS, q_gain, position_all).astype(jnp.bfloat16)
    own_rows = lax.dynamic_index_in_dim(
        projected[:, Q_DIM:].reshape(pages_dev, narrow_count, rows_page, KV_DIM),
        narrow_index,
        1,
        keepdims=False,
    ).reshape(slice_rows, KV_DIM)
    keys_own = rotate(own_rows[:, :key_width], KV_HEADS, k_gain, position_own).astype(jnp.bfloat16)
    values_own = own_rows[:, key_width:].astype(jnp.bfloat16)
    cache_rows = jnp.concatenate([keys_own, values_own], axis=1).reshape(
        pages_dev, rows_page, KV_DIM
    )
    paged_cache = jnp.zeros_like(cache_rows).at[page_table].set(cache_rows)
    query_groups = queries.reshape(tokens_dev, KV_HEADS, GROUP, HEAD)
    key_block = lax.all_gather(keys_own, "wide", axis=0, tiled=True)
    value_block = lax.all_gather(values_own, "wide", axis=0, tiled=True)
    key_count = key_block.shape[0]
    row_index = jnp.arange(key_count, dtype=jnp.int32)
    shard_index = row_index // slice_rows
    inner_index = row_index % slice_rows
    key_tokens = (
        shard_index * tokens_dev
        + inner_index // rows_page * PAGE
        + narrow_index * rows_page
        + inner_index % rows_page
    )
    key_segment, unused = token_place(key_tokens, lengths)
    visible = (key_segment[None, :] == segment_all[:, None]) & (
        key_tokens[None, :] <= all_tokens[:, None]
    )
    scores = (
        jnp.einsum(
            "tkgd,nkd->tkgn",
            query_groups,
            key_block.reshape(key_count, KV_HEADS, HEAD),
            preferred_element_type=jnp.float32,
        )
        * scale
    )
    weights = jnp.where(visible[:, None, None, :], jnp.exp(scores), 0.0)
    numerator = jnp.einsum(
        "tkgn,nkd->tkgd",
        weights.astype(jnp.bfloat16),
        value_block.reshape(key_count, KV_HEADS, HEAD),
        preferred_element_type=jnp.float32,
    )
    denominator = jnp.sum(weights, axis=-1)
    numerator, denominator = (numerator, denominator)
    numerator, denominator = lax.psum((numerator, denominator), "narrow")
    attended = (numerator / denominator[..., None]).reshape(tokens_dev, Q_DIM).astype(jnp.bfloat16)
    mixed_rows = jnp.dot(
        attended,
        lax.all_gather(out_weight, "wide", axis=0, tiled=True),
        preferred_element_type=jnp.float32,
    )
    hidden_out = (input_values + mixed_rows).astype(jnp.bfloat16)
    return (hidden_out, paged_cache)


def solution(mesh):
    return jax.shard_map(
        on_device,
        mesh=mesh,
        in_specs=(
            P("wide", "narrow"),
            P("narrow"),
            P("narrow", "wide"),
            P(),
            P(),
            P("wide", "narrow"),
            P(),
            P("wide"),
        ),
        out_specs=(P("wide", "narrow"), P("wide", "narrow", None)),
        check_vma=False,
    )
```

profile of v0, /device:TPU:32, one launch (start us, length us, event | category | flops | bytes accessed | tf_op | source)
XLA Modules:
  0.0 860.2 jit_solution(7487213716153726544)
XLA Ops:
  7.2 229.6 %all-gather = bf16[64,30,256]{2,1,0:T(8,128)(2,1)S(1)} all-gather(bf16[1,30,256]{2,1,0:T(8,128)(2,1)} %bitcast.51), channel_id=1, replica_groups=mesh['wide'=64,'narrow'=8] {'wide'}, dimensions={0}, use_global_device_ids=true | all-gather | bytes 998400 | tf_op jit(solution)/shard_map/all_gather | solution.py:66
  236.8 0.3 reshape.393
  237.1 1.8 fusion.11
  238.9 0.6 copy-done.8
  239.7 0.2 reduce-window.8
  239.9 0.1 fusion.10
  240.0 13.7 %psum.29 = f32[256]{0:T(256)S(1)} all-reduce(f32[256]{0:T(256)S(1)} %fusion.10), channel_id=1, replica_groups=mesh['wide'=64,'narrow'=8] {'narrow'}, use_global_device_ids=true, to_apply=%region_2.3 | all-reduce | flops 256 | bytes 2048 | tf_op jit(solution)/shard_map/psum | solution.py:79
  253.9 0.1 multiply_cosine_fusion.1
  254.1 61.9 %all-reduce.3.cloned.1.call-done = f32[256,1920]{1,0:T(8,128)} async-done(((f32[256,1920]{1,0:T(8,128)}), f32[256,1920]{1,0:T(8,128)}) %all-reduce.3.cloned.1.call-update) | async-done | bytes 1966096 | tf_op jit(solution)/shard_map/psum | solution.py:79
  316.0 1.7 broadcast_multiply_fusion
  318.1 0.1 subtract_convert_fusion.1
  318.4 0.7 convert_element_type.68
  319.1 0.5 convert_element_type.69
  320.0 0.2 multiply_cosine_fusion
  320.2 2.3 compare_and_fusion
  322.5 0.7 slice.50
  323.2 0.4 copy.31
  323.6 0.1 multiply_reduce_fusion
  323.9 0.3 multiply_multiply_fusion
  324.2 0.2 subtract_convert_fusion
  324.4 122.7 %all-gather.7.cloned.1.call-done = bf16[2048,320]{1,0:T(8,128)(2,1)} async-done(((bf16[32,320]{1,0:T(8,128)(2,1)}), bf16[2048,320]{1,0:T(8,128)(2,1)}) %all-gather.7.cloned.1.call-update) | async-done | bytes 1310736 | tf_op jit(solution)/shard_map/all_gather | solution.py:96
  447.1 1.7 copy.30
  448.8 15.7 %fusion = (f32[256,5,4]{0,2,1:T(4,128)S(1)}, f32[5,2048,256,4]{2,1,3,0:T(8,128)}) fusion(pred[256,2048]{0,1:T(8,128)(4,1)S(1)} %copy-done.1, bf16[2048,5,64,1]{0,2,3,1:T(8,128)(2,1)S(1)} %bitcast.46, bf16[256,5,4,64]{0,3,2,1:T(8,128)(2,1)S(1)} %bitcast.49), kind=kOutput, calls=%fused_computation.2 | convolution fusion | flops 1373629440 | bytes 44453888 | tf_op jit(solution)/shard_map/tkgd,nkd->tkgn/dot_general | solution.py:113
  464.5 114.4 %all-gather.5.cloned.1.call-done = bf16[2048,320]{1,0:T(8,128)(2,1)} async-done(((bf16[32,320]{1,0:T(8,128)(2,1)}), bf16[2048,320]{1,0:T(8,128)(2,1)}) %all-gather.5.cloned.1.call-update) | async-done | bytes 1310736 | tf_op jit(solution)/shard_map/all_gather | solution.py:97
  578.9 1.7 copy.29
  580.6 17.4 %fusion.5 = f32[256,5,4,64]{0,3,2,1:T(8,128)} fusion(bf16[2048,5,64,1]{0,2,3,1:T(8,128)(2,1)S(1)} %bitcast.47, f32[5,2048,256,4]{2,1,3,0:T(8,128)} %get-tuple-element.11, pred[256,2048]{0,1:T(8,128)(4,1)S(1)} %copy-done.1), kind=kOutput, calls=%fused_computation.7 | convolution fusion | flops 1373634560 | bytes 45088768 | tf_op jit(solution)/shard_map/tkgn,nkd->tkgd/dot_general | solution.py:122
  598.0 226.0 %all-gather.1 = bf16[64,20,256]{2,1,0:T(8,128)(2,1)S(1)} all-gather(bf16[1,20,256]{2,1,0:T(8,128)(2,1)S(1)} %bitcast.52), channel_id=1, replica_groups=mesh['wide'=64,'narrow'=8] {'wide'}, dimensions={0}, use_global_device_ids=true | all-gather | bytes 665600 | tf_op jit(solution)/shard_map/all_gather | solution.py:134
  824.0 0.1 reshape.395
  824.3 0.6 scatter_fusion
  825.0 26.2 %psum.31 = f32[256,5,4]{0,2,1:T(4,128)S(1)} all-reduce(f32[256,5,4]{0,2,1:T(4,128)S(1)} %get-tuple-element.10), channel_id=1, replica_groups=mesh['wide'=64,'narrow'=8] {'narrow'}, use_global_device_ids=true, to_apply=%region_13.14 | all-reduce | flops 5120 | bytes 40960 | tf_op jit(solution)/shard_map/psum | solution.py:130
  851.2 1.5 divide_convert_fusion
  852.6 1.0 fusion.8
  (63 shorter events, 1.6 us)
Async XLA Ops:
  7.2 229.9 %copy-start.7 = (bf16[256]{0:T(256)(128)(2,1)S(1)}, bf16[256]{0:T(256)(128)(2,1)}, u32[]{:S(2)}) copy-start(bf16[256]{0:T(256)(128)(2,1)} %param.9) | copy-start | bytes 1540
  7.2 229.9 %copy-start = (bf16[256,256]{1,0:T(8,128)(2,1)S(1)}, bf16[256,256]{1,0:T(8,128)(2,1)}, u32[]{:S(2)}) copy-start(bf16[256,256]{1,0:T(8,128)(2,1)} %param.8) | copy-start | bytes 393220
  7.2 308.8 %all-reduce.3.cloned.1.call-start = ((), (), s32[]{:S(2)}) async-start(), calls=%async_computation | async-start | bytes 3932160 | tf_op jit(solution)/shard_map/psum | solution.py:79
  238.9 0.7 copy-start.8
  238.9 0.8 copy-start.9
  238.9 208.2 %all-gather.7.cloned.1.call-start = ((), (), s32[]{:S(2)}) async-start(), calls=%async_computation.2 | async-start | bytes 1597440 | tf_op jit(solution)/shard_map/all_gather | solution.py:96
  317.7 1.4 copy-start.10
  319.1 259.8 %all-gather.5.cloned.1.call-start = ((), (), s32[]{:S(2)}) async-start(), calls=%async_computation.1 | async-start | bytes 1597440 | tf_op jit(solution)/shard_map/all_gather | solution.py:97
  323.2 0.6 copy-start.6
  323.8 527.4 %all-reduce.5.cloned.1.call-start = ((), (), s32[]{:S(2)}) async-start(), calls=%async_computation.3 | async-start | bytes 2621440 | tf_op jit(solution)/shard_map/psum | solution.py:130
  324.4 124.4 %copy-start.1 = (pred[256,2048]{0,1:T(8,128)(4,1)S(1)}, pred[256,2048]{0,1:T(8,128)(4,1)}, u32[]{:S(2)}) copy-start(pred[256,2048]{0,1:T(8,128)(4,1)} %compare_and_fusion) | copy-start | bytes 1572868
  580.5 17.5 %copy-start.5 = (bf16[20,256]{1,0:T(8,128)(2,1)S(1)}, bf16[20,256]{1,0:T(8,128)(2,1)}, u32[]{:S(2)}) copy-start(bf16[20,256]{1,0:T(8,128)(2,1)} %param.13) | copy-start | bytes 30724
  598.0 226.2 %copy-start.11 = (s32[4]{0:T(128)S(1)}, s32[4]{0:T(128)}, u32[]{:S(2)}) copy-start(s32[4]{0:T(128)} %param.15) | copy-start | bytes 52
  598.0 226.2 %copy-start.2 = (bf16[32,320]{1,0:T(8,128)(2,1)S(1)}, bf16[32,320]{1,0:T(8,128)(2,1)}, u32[]{:S(2)}) copy-start(bf16[32,320]{1,0:T(8,128)(2,1)} %slice.50) | copy-start | bytes 61444
  598.0 226.2 %copy-start.3 = (bf16[32,320]{1,0:T(8,128)(2,1)S(1)}, bf16[32,320]{1,0:T(8,128)(2,1)}, u32[]{:S(2)}) copy-start(bf16[32,320]{1,0:T(8,128)(2,1)} %convert_element_type.68) | copy-start | bytes 61444
  825.0 28.7 %copy-start.4 = (bf16[4,8,640]{2,1,0:T(8,128)(2,1)}, bf16[4,8,640]{2,1,0:T(8,128)(2,1)S(1)}, u32[]{:S(2)}) copy-start(bf16[4,8,640]{2,1,0:T(8,128)(2,1)S(1)} %scatter_fusion) | copy-start | bytes 122884
Sparse Core Ops, SparseCore 0:
  239.0 76.9 all-reduce.2
  321.9 125.1 all-gather.6
  453.1 125.7 all-gather.4
  598.1 81.6 all-reduce.4
where the time goes:
time: 861 us; the launch traced here: 860 us
  blocking collectives  496 us (58%)
  waiting for transfers between devices  299 us (35%)
  matrix products  35.9 us (4%)
  between operations  14.1 us (2%)
    all_gather x1, blocking collectives, on_device(): lax.all_gather(qkv_weight, 'wide', axis=1, tiled=True)  230 us
    all_gather x1, blocking collectives, on_device(): lax.all_gather(out_weight, 'wide', axis=0, tiled=True)  226 us
    all_gather x1, waiting for transfers between devices, on_device(): key_block = lax.all_gather(keys_own, 'wide', axis=0, tiled=True)  123 us
    all_gather x1, waiting for transfers between devices, on_device(): value_block = lax.all_gather(values_own, 'wide', axis=0, tiled=True)  114 us
    psum x1, waiting for transfers between devices, on_device(): summed, squares = lax.psum((partial_sums, square_part), 'narrow')  61.9 us
    psum x1, blocking collectives, on_device(): numerator, denominator = lax.psum((numerator, denominator), 'narrow')  26.2 us
    dot_general x1, matrix products, on_device(): jnp.einsum('tkgn,nkd->tkgd', weights.astype(jnp.bfloat16), value_block.re...  17.4 us
  transfers between devices with their start and end apart: 4, of which 3 were waited for; matrix products, arithmetic and copies ran while one was open for 3% of the time, Pallas kernels for 0%

commit v1 on v0

--- a/solution.py
+++ b/solution.py
@@ -94,7 +94,10 @@
     paged_cache = jnp.zeros_like(cache_rows).at[page_table].set(cache_rows)
     query_groups = queries.reshape(tokens_dev, KV_HEADS, GROUP, HEAD)
     key_block = lax.all_gather(keys_own, "wide", axis=0, tiled=True)
-    value_block = lax.all_gather(values_own, "wide", axis=0, tiled=True)
+    work_now = jax.lax.psum(1, axis_name="wide")
+    frame_out = jnp.stack([values_own] * work_now)
+    local_part = jax.lax.all_to_all(frame_out, "wide", 0, 0)
+    value_block = jnp.concatenate(local_part, axis=0)
     key_count = key_block.shape[0]
     row_index = jnp.arange(key_count, dtype=jnp.int32)
     shard_index = row_index // slice_rows

time: 861 us -> 769 us (0.89)
  waiting for transfers between devices: 299 us -> 187 us
  starting transfers between devices: 0.16 us -> 15.9 us
    all_gather x1 -> x0, waiting for transfers between devices: 114 us -> none  [on_device(): value_block = lax.all_gather(values_own, 'wide', axis=0, tiled=True)]
    all_to_all x0 -> x1, starting transfers between devices: none -> 15.8 us  [on_device(): local_part = jax.lax.all_to_all(frame_out, 'wide', 0, 0)]
  transfers between devices with their start and end apart: 4 -> 4, of which waited for: 3 -> 2; matrix products, arithmetic and copies ran while one was open for 3% -> 3% of each run, Pallas kernels for 0% -> 0%
where the time goes in v1:
time: 769 us
  blocking collectives  496 us (64%)
  waiting for transfers between devices  187 us (24%)
  matrix products  38.8 us (5%)
  starting transfers between devices  15.9 us (2%)
  between operations  14.1 us (2%)
  local copies, waits for them, and re-layouts  8.76 us (1%)
  other arithmetic  7.83 us (1%)
    all_gather x1, blocking collectives, on_device(): lax.all_gather(qkv_weight, 'wide', axis=1, tiled=True)  230 us
    all_gather x1, blocking collectives, on_device(): lax.all_gather(out_weight, 'wide', axis=0, tiled=True)  226 us
    all_gather x1, waiting for transfers between devices, on_device(): key_block = lax.all_gather(keys_own, 'wide', axis=0, tiled=True)  125 us
    psum x1, waiting for transfers between devices, on_device(): summed, squares = lax.psum((partial_sums, square_part), 'narrow')  62.5 us
    psum x1, blocking collectives, on_device(): numerator, denominator = lax.psum((numerator, denominator), 'narrow')  26.7 us
    dot_general x1, matrix products, on_device(): jnp.einsum('tkgn,nkd->tkgd', weights.astype(jnp.bfloat16), value_block.re...  18.9 us
    dot_general x1, matrix products, on_device(): jnp.einsum('tkgd,nkd->tkgn', query_groups, key_block.reshape(key_count, K...  17.2 us
    all_to_all x1, starting transfers between devices, on_device(): local_part = jax.lax.all_to_all(frame_out, 'wide', 0, 0)  15.8 us
  transfers between devices with their start and end apart: 4, of which 2 were waited for; matrix products, arithmetic and copies ran while one was open for 3% of the time, Pallas kernels for 0%

profile of v1, /device:TPU:32, one launch (start us, length us, event | category | flops | bytes accessed | tf_op | source)
XLA Modules:
  0.0 768.8 jit_solution(4996524667803514727)
XLA Ops:
  7.2 229.6 %all-gather = bf16[64,30,256]{2,1,0:T(8,128)(2,1)S(1)} all-gather(bf16[1,30,256]{2,1,0:T(8,128)(2,1)} %bitcast.46), channel_id=1, replica_groups=mesh['wide'=64,'narrow'=8] {'wide'}, dimensions={0}, use_global_device_ids=true | all-gather | bytes 998400 | tf_op jit(solution)/shard_map/all_gather | solution.py:66
  236.8 0.3 reshape.391
  237.1 1.8 fusion.14
  239.2 0.2 reduce-window.8
  239.3 0.1 fusion.13
  239.5 13.8 %psum.29 = f32[256]{0:T(256)S(1)} all-reduce(f32[256]{0:T(256)S(1)} %fusion.13), channel_id=1, replica_groups=mesh['wide'=64,'narrow'=8] {'narrow'}, use_global_device_ids=true, to_apply=%region_2.3 | all-reduce | flops 256 | bytes 2048 | tf_op jit(solution)/shard_map/psum | solution.py:79
  253.5 0.1 multiply_cosine_fusion.1
  253.6 62.5 %all-reduce.3.cloned.1.call-done = f32[256,1920]{1,0:T(8,128)} async-done(((f32[256,1920]{1,0:T(8,128)}), f32[256,1920]{1,0:T(8,128)}) %all-reduce.3.cloned.1.call-update) | async-done | bytes 1966096 | tf_op jit(solution)/shard_map/psum | solution.py:79
  316.1 1.7 broadcast_multiply_fusion
  318.0 0.1 multiply_reduce_fusion.1
  318.1 0.1 multiply_multiply_fusion.1
  318.2 0.1 subtract_convert_fusion.1
  318.5 0.7 convert_element_type.68
  319.5 0.2 multiply_cosine_fusion
  319.7 2.3 compare_and_fusion
  322.2 0.4 copy.30
  322.6 1.3 stack.2
  323.9 15.8 %all-to-all-start = ((bf16[64,32,320]{2,1,0:T(8,128)(2,1)}), bf16[64,32,320]{2,1,0:T(8,128)(2,1)S(1)}, u32[]{:S(2)}, u32[]{:S(2)}) async-start(bf16[64,32,320]{2,1,0:T(8,128)(2,1)} %stack.2), calls=%async_computation | async-start | bytes 3145728 | tf_op jit(solution)/shard_map/all_to_all | solution.py:99
  339.7 0.1 multiply_reduce_fusion
  339.9 0.3 multiply_multiply_fusion
  340.2 0.2 subtract_convert_fusion
  340.4 124.5 %all-gather.4.cloned.1.call-done = bf16[2048,320]{1,0:T(8,128)(2,1)} async-done(((bf16[32,320]{1,0:T(8,128)(2,1)}), bf16[2048,320]{1,0:T(8,128)(2,1)}) %all-gather.4.cloned.1.call-update) | async-done | bytes 1310736 | tf_op jit(solution)/shard_map/all_gather | solution.py:96
  464.9 1.7 copy.29
  466.6 17.2 %fusion = (f32[256,5,4]{0,2,1:T(4,128)}, f32[5,2048,256,4]{2,1,3,0:T(8,128)}) fusion(pred[256,2048]{0,1:T(8,128)(4,1)} %compare_and_fusion, bf16[2048,5,64,1]{0,2,3,1:T(8,128)(2,1)S(1)} %bitcast.42, bf16[256,5,4,64]{0,3,2,1:T(8,128)(2,1)S(1)} %bitcast.44), kind=kOutput, calls=%fused_computation.2 | convolution fusion | flops 1373629440 | bytes 44453888 | tf_op jit(solution)/shard_map/tkgd,nkd->tkgn/dot_general | solution.py:116
  483.8 3.2 reshape_reshape.3
  487.0 18.9 %fusion.6 = f32[256,5,4,64]{0,3,2,1:T(8,128)} fusion(f32[5,2048,256,4]{2,1,3,0:T(8,128)} %get-tuple-element.11, pred[256,2048]{0,1:T(8,128)(4,1)S(1)} %copy-done.2, bf16[2048,5,64,1]{2,1,0,3:T(8,128)(2,1)} %bitcast.41), kind=kOutput, calls=%fused_computation.8 | convolution fusion | flops 1373634560 | bytes 45088768 | tf_op jit(solution)/shard_map/tkgn,nkd->tkgd/dot_general | solution.py:125
  505.9 226.2 %all-gather.1 = bf16[64,20,256]{2,1,0:T(8,128)(2,1)S(1)} all-gather(bf16[1,20,256]{2,1,0:T(8,128)(2,1)S(1)} %bitcast.47), channel_id=1, replica_groups=mesh['wide'=64,'narrow'=8] {'wide'}, dimensions={0}, use_global_device_ids=true | all-gather | bytes 665600 | tf_op jit(solution)/shard_map/all_gather | solution.py:137
  732.1 0.1 reshape.393
  732.4 0.6 scatter_fusion
  733.0 26.7 %psum.31 = f32[256,5,4]{0,2,1:T(4,128)S(1)} all-reduce(f32[256,5,4]{0,2,1:T(4,128)S(1)} %copy-done.7), channel_id=1, replica_groups=mesh['wide'=64,'narrow'=8] {'narrow'}, use_global_device_ids=true, to_apply=%region_13.14 | all-reduce | flops 5120 | bytes 40960 | tf_op jit(solution)/shard_map/psum | solution.py:133
  759.7 1.5 divide_convert_fusion
  761.2 1.0 fusion.11
  (67 shorter events, 1.5 us)
Async XLA Ops:
  7.2 229.9 %copy-start.9 = (bf16[256]{0:T(256)(128)(2,1)S(1)}, bf16[256]{0:T(256)(128)(2,1)}, u32[]{:S(2)}) copy-start(bf16[256]{0:T(256)(128)(2,1)} %param.9) | copy-start | bytes 1540
  7.2 229.9 %copy-start = (bf16[256,256]{1,0:T(8,128)(2,1)S(1)}, bf16[256,256]{1,0:T(8,128)(2,1)}, u32[]{:S(2)}) copy-start(bf16[256,256]{1,0:T(8,128)(2,1)} %param.8) | copy-start | bytes 393220
  7.2 308.9 %all-reduce.3.cloned.1.call-start = ((), (), s32[]{:S(2)}) async-start(), calls=%async_computation.1 | async-start | bytes 3932160 | tf_op jit(solution)/shard_map/psum | solution.py:79
  237.1 1.9 copy-start.10
  237.1 2.0 copy-start.11
  238.9 226.0 %all-gather.4.cloned.1.call-start = ((), (), s32[]{:S(2)}) async-start(), calls=%async_computation.2 | async-start | bytes 1597440 | tf_op jit(solution)/shard_map/all_gather | solution.py:96
  317.8 1.4 copy-start.12
  322.2 1.7 copy-start.4
  323.9 160.0 %all-to-all-start = ((bf16[64,32,320]{2,1,0:T(8,128)(2,1)}), bf16[64,32,320]{2,1,0:T(8,128)(2,1)S(1)}, u32[]{:S(2)}, u32[]{:S(2)}) async-start(bf16[64,32,320]{2,1,0:T(8,128)(2,1)} %stack.2), calls=%async_computation | async-start | bytes 3145728 | tf_op jit(solution)/shard_map/all_to_all | solution.py:99
  339.7 420.1 %all-reduce.5.cloned.1.call-start = ((), (), s32[]{:S(2)}) async-start(), calls=%async_computation.3 | async-start | bytes 2621440 | tf_op jit(solution)/shard_map/psum | solution.py:133
  483.8 3.2 copy-start.2
  487.0 18.9 %copy-start.8 = (bf16[20,256]{1,0:T(8,128)(2,1)S(1)}, bf16[20,256]{1,0:T(8,128)(2,1)}, u32[]{:S(2)}) copy-start(bf16[20,256]{1,0:T(8,128)(2,1)} %param.13) | copy-start | bytes 30724
  505.8 226.4 %copy-start.13 = (s32[4]{0:T(128)S(1)}, s32[4]{0:T(128)}, u32[]{:S(2)}) copy-start(s32[4]{0:T(128)} %param.15) | copy-start | bytes 52
  505.8 226.4 %copy-start.3 = (bf16[32,320]{1,0:T(8,128)(2,1)S(1)}, bf16[32,320]{1,0:T(8,128)(2,1)}, u32[]{:S(2)}) copy-start(bf16[32,320]{1,0:T(8,128)(2,1)} %convert_element_type.68) | copy-start | bytes 61444
  505.9 226.4 %copy-start.5 = (bf16[32,320]{1,0:T(8,128)(2,1)S(1)}, bf16[32,320]{1,0:T(8,128)(2,1)}, u32[]{:S(2)}) copy-start(bf16[32,320]{1,0:T(8,128)(2,1)} %copy-done.4) | copy-start | bytes 61444
  505.9 227.2 %copy-start.7 = (f32[256,5,4]{0,2,1:T(4,128)S(1)}, f32[256,5,4]{0,2,1:T(4,128)}, u32[]{:S(2)}) copy-start(f32[256,5,4]{0,2,1:T(4,128)} %get-tuple-element.10) | copy-start | bytes 61444
  732.1 29.1 %copy-start.1 = (bf16[256,256]{1,0:T(8,128)(2,1)S(1)}, bf16[256,256]{1,0:T(8,128)(2,1)}, u32[]{:S(2)}) copy-start(bf16[256,256]{1,0:T(8,128)(2,1)} %param.8) | copy-start | bytes 393220
  733.0 29.3 %copy-start.6 = (bf16[4,8,640]{2,1,0:T(8,128)(2,1)}, bf16[4,8,640]{2,1,0:T(8,128)(2,1)S(1)}, u32[]{:S(2)}) copy-start(bf16[4,8,640]{2,1,0:T(8,128)(2,1)S(1)} %scatter_fusion) | copy-start | bytes 122884
Sparse Core Ops, SparseCore 0:
  239.0 77.0 all-reduce.2
  322.0 142.8 all-gather.3
  506.0 81.5 all-reduce.4
